TPU v7x, 512 devices: a whole 4x4x16 slice. The times are simulated.
512 devices in a mesh: replica: 8 (over y, x_lo), mp: 64 (over z, x_hi, core).
Axes of the slice: x: 4 (x_hi: 2, x_lo: 2; x = x_hi * 2 + x_lo), y: 4, z: 16, core: 2. Of those that a mesh axis runs over, the one named last changes fastest.
Arguments:
- owner_shard: int32 [1024, 256], P(('replica', 'mp')), may hold values from 0 to 63, as said below
- slot_index: int32 [1024, 256], P(('replica', 'mp')), may hold values from 0 to 127
- lengths: int32 [1024], P(('replica', 'mp')), may hold values from 32 to 256
- labels: float32 [1024, 256], P(('replica', 'mp')), may hold values from 0 to 1
- embed_table: bfloat16 [131072, 256], P('mp'), may hold values from -3 to 3
- accumulator: float32 [131072], P('mp'), may hold values from 0.1 to 10
- touched: int32 [8192], P('mp'), may hold values from 0 to 2047, as said below
- w_in: bfloat16 [256, 1024], replicated, may hold values from -0.375 to 0.375
- w_mid: bfloat16 [1024, 1024], replicated, may hold values from -0.1875 to 0.1875
- norm_gain: float32 [1024], replicated, may hold values from 0.5 to 2
- w_out: float32 [1024], replicated, may hold values from -0.1875 to 0.1875
Outputs:
- table_out: bfloat16 [131072, 256], P('mp')
- accum_out: float32 [131072], P('mp')
Inputs may be any that keep to these rules, and one draw needn't show every extreme that they name: `owner_shard`: among the events of one device, every shard is named at most 16 times, and one shard, the same for all devices, is named exactly 16 times by every device. `touched`: the 128 entries of each shard are distinct rows of that shard.
All inputs are finite; a program needn't handle non-finite values.
Results may differ from a plain program's by a relative error of at most 0.0034.
Values may be sent and summed in bfloat16 or wider, within the bound.
A program may use at most 64 MiB of HBM per device.

v0:
```python
import jax
import jax.numpy as jnp
from jax import lax
from jax.sharding import PartitionSpec as P

learn_rate = 1.0


def silu_slope(values):
    sigma_val = jax.nn.sigmoid(values)
    return sigma_val * (1.0 + values * (1.0 - sigma_val))


def encoder_grad(looked_up, labels, live_mask, w_in, w_mid, norm_gain, w_out):
    pre_act = jnp.dot(looked_up, w_in, preferred_element_type=jnp.float32)
    hidden = jax.nn.silu(pre_act)
    inv_rms = lax.rsqrt(jnp.mean(hidden * hidden, axis=-1, keepdims=True) + 1e-06)
    normed = (hidden * inv_rms * norm_gain).astype(jnp.bfloat16)
    mixed = jnp.dot(normed, w_mid, preferred_element_type=jnp.float32)
    output = hidden + jax.nn.silu(mixed)
    logits = jnp.sum(output * w_out, axis=-1)
    d_logit = (jax.nn.sigmoid(logits) - labels) * live_mask
    d_output = d_logit[:, None] * w_out
    d_mixed = (d_output * silu_slope(mixed)).astype(jnp.bfloat16)
    d_normed = jnp.dot(d_mixed, w_mid.T, preferred_element_type=jnp.float32)
    gained = d_normed * norm_gain
    d_hidden = (
        d_output
        + inv_rms * gained
        - hidden * inv_rms**3 * jnp.mean(hidden * gained, axis=-1, keepdims=True)
    )
    d_pre = (d_hidden * silu_slope(pre_act)).astype(jnp.bfloat16)
    return jnp.dot(d_pre, w_in.T, preferred_element_type=jnp.float32).astype(jnp.bfloat16)


def adagrad_rows(grad_rows_in, old_rows, old_acc):
    acc_new = old_acc + jnp.sum(grad_rows_in * grad_rows_in, axis=1)
    new_rows = (
        old_rows.astype(jnp.float32) - learn_rate * grad_rows_in * lax.rsqrt(acc_new)[:, None]
    )
    return (new_rows, acc_new)


def on_device(
    owner_shard,
    slot_index,
    lengths,
    labels,
    embed_table,
    accumulator,
    touched,
    w_in,
    w_mid,
    norm_gain,
    w_out,
):
    mp_count = lax.axis_size("mp")
    samples, length = owner_shard.shape
    events = samples * length
    capacity = max(2, 2 * events // mp_count)
    emb_width = embed_table.shape[1]
    touch_count = touched.shape[0]
    owners = owner_shard.reshape(events)
    slots = slot_index.reshape(events)
    live_mask = (
        (jnp.arange(length, dtype=jnp.int32)[None, :] < lengths[:, None])
        .astype(jnp.float32)
        .reshape(events)
    )
    local_block = embed_table[touched]
    owner_onehot = (owners[:, None] == jnp.arange(mp_count, dtype=jnp.int32)[None, :]).astype(
        jnp.int32
    )
    slot_rank = jnp.sum((jnp.cumsum(owner_onehot, axis=0) - 1) * owner_onehot, axis=1)
    send_pos = owners * capacity + slot_rank
    requests = (
        jnp.full((mp_count * capacity,), -1, jnp.int32)
        .at[send_pos]
        .set(slots)
        .reshape(mp_count, capacity)
    )
    every_block = lax.all_gather(local_block, "mp", axis=0, tiled=True)
    looked_up = every_block[owners * touch_count + slots]
    asked_slots = lax.all_to_all(requests, "mp", split_axis=0, concat_axis=0, tiled=True)
    block_rows = min(events, 512)
    block_count = events // block_rows

    def one_block(pieces):
        return encoder_grad(pieces[0], pieces[1], pieces[2], w_in, w_mid, norm_gain, w_out)

    event_grads = lax.map(
        one_block,
        (
            looked_up.reshape(block_count, block_rows, emb_width),
            labels.reshape(block_count, block_rows),
            live_mask.reshape(block_count, block_rows),
        ),
    ).reshape(events, emb_width)
    outgoing = (
        jnp.zeros((mp_count * capacity, emb_width), jnp.bfloat16)
        .at[send_pos]
        .set(event_grads)
        .reshape(mp_count, capacity, emb_width)
    )
    incoming = lax.all_to_all(outgoing, "mp", split_axis=0, concat_axis=0, tiled=True)
    slot_onehot = (
        asked_slots.reshape(-1)[:, None] == jnp.arange(touch_count, dtype=jnp.int32)[None, :]
    ).astype(jnp.bfloat16)
    grad_block = jnp.einsum(
        "rt,re->te",
        slot_onehot,
        incoming.reshape(-1, emb_width),
        preferred_element_type=jnp.float32,
    )
    touched_acc = accumulator[touched]
    grad_total = lax.psum(grad_block, "replica")
    new_rows, new_acc = adagrad_rows(grad_total, local_block, touched_acc)
    table_out = embed_table.at[touched].set(new_rows.astype(jnp.bfloat16))
    accum_out = accumulator.at[touched].set(new_acc)
    return (table_out, accum_out)


def solution(mesh):
    in_specs = (
        P(("replica", "mp"), None),
        P(("replica", "mp"), None),
        P(("replica", "mp")),
        P(("replica", "mp"), None),
        P("mp", None),
        P("mp"),
        P("mp"),
        P(),
        P(),
        P(),
        P(),
    )
    out_specs = (P("mp", None), P("mp"))
    return jax.shard_map(
        on_device, mesh=mesh, in_specs=in_specs, out_specs=out_specs, check_vma=False
    )
```

profile of v0, /device:TPU:4, one launch (start us, length us, event | category | flops | bytes accessed | tf_op | source)
XLA Modules:
  0.0 320.2 jit_solution(12716276199991593378)
XLA Ops:
  7.3 1.4 copy.28
  8.7 1.5 gather_fusion
  10.3 1.2 reduce-window.6
  11.9 2.4 scatter_custom_fusion
  14.3 0.7 all_to_all.9
  15.0 18.6 %all-to-all-start = ((s32[64,1,16]{2,1,0:T(1,128)}), s32[64,1,16]{2,1,0:T(1,128)S(1)}, u32[]{:S(2)}, u32[]{:S(2)}) async-start(s32[64,1,16]{2,1,0:T(1,128)} %bitcast.3), calls=%async_computation | async-start | bytes 65536 | tf_op jit(solution)/shard_map/all_to_all | solution.py:84
  33.8 130.6 %all-gather.3.cloned.1.call-done = bf16[8192,256]{1,0:T(8,128)(2,1)} async-done(((bf16[128,256]{1,0:T(8,128)(2,1)}), bf16[8192,256]{1,0:T(8,128)(2,1)}) %all-gather.3.cloned.1.call-update) | async-done | bytes 4194320 | tf_op jit(solution)/shard_map/all_gather | solution.py:82
  164.3 4.3 %gather_fusion.1 = bf16[512,256]{1,0:T(8,128)(2,1)S(1)} fusion(bf16[8192,256]{1,0:T(8,128)(2,1)} %all-gather.3.cloned.1.call-done, s32[1024]{0:T(1024)S(1)} %pad_clamp_fusion), kind=kCustom, calls=%fused_computation.1 | custom fusion | bytes 526336 | tf_op jit(solution)/shard_map/gather | solution.py:83
  168.6 1.9 multiply_reduce_fusion.2
  170.6 2.3 multiply_reduce_fusion.1
  172.9 2.0 multiply_reduce_fusion
  174.9 2.4 convolution_convert_fusion
  177.3 3.5 %scatter_custom_fusion.1 = bf16[1024,256]{1,0:T(8,128)(2,1)} fusion(s32[512]{0:T(512)S(1)} %bitcast.53, bf16[512,256]{1,0:T(8,128)(2,1)} %convolution_convert_fusion, bf16[]{:T(256)} %constant.35.clone.1), kind=kCustom, calls=%fused_computation.30 | custom fusion | bytes 524800 | tf_op jit(solution)/shard_map/scatter | solution.py:102
  180.9 10.8 %all-to-all-start.1 = ((bf16[64,16,256]{2,1,0:T(8,128)(2,1)}), bf16[64,16,256]{2,1,0:T(8,128)(2,1)}, u32[]{:S(2)}, u32[]{:S(2)}) async-start(bf16[64,16,256]{2,1,0:T(8,128)(2,1)} %bitcast.43), calls=%async_computation.1 | async-start | bytes 1048576 | tf_op jit(solution)/shard_map/all_to_all | solution.py:105
  191.7 0.5 broadcast.180
  192.2 0.7 reduce.5
  193.1 32.1 %all-to-all-done.1 = bf16[64,16,256]{2,1,0:T(8,128)(2,1)} async-done(((bf16[64,16,256]{2,1,0:T(8,128)(2,1)}), bf16[64,16,256]{2,1,0:T(8,128)(2,1)}, u32[]{:S(2)}, u32[]{:S(2)}) %all-to-all-start.1) | async-done | bytes 524320 | tf_op jit(solution)/shard_map/all_to_all | solution.py:105
  225.2 2.2 fusion.14
  227.4 1.1 gather_fusion.2
  228.5 79.6 %all-reduce.2.cloned.1.call-done = f32[128,256]{1,0:T(8,128)} async-done(((f32[128,256]{1,0:T(8,128)}), f32[128,256]{1,0:T(8,128)}) %all-reduce.2.cloned.1.call-update) | async-done | bytes 131088 | tf_op jit(solution)/shard_map/psum | solution.py:116
  308.2 1.0 multiply_reduce_fusion.3
  309.2 1.0 scatter_fusion
  310.2 2.1 scatter_custom_fusion.2
  312.4 1.0 copy-done.2
  (55 shorter events, 0.9 us)
Async XLA Ops:
  7.2 163.4 %copy-start = (bf16[1024,1024]{1,0:T(8,128)(2,1)S(1)}, bf16[1024,1024]{1,0:T(8,128)(2,1)}, u32[]{:S(2)}) copy-start(bf16[1024,1024]{1,0:T(8,128)(2,1)} %param.19) | copy-start | bytes 6291460
  7.2 3.0 copy-start.4
  7.2 3.0 copy-start.6
  7.2 26.4 %copy-start.12 = (s32[2]{0:T(128)S(1)}, s32[2]{0:T(128)}, u32[]{:S(2)}) copy-start(s32[2]{0:T(128)} %param.13) | copy-start | bytes 28
  7.2 26.5 %copy-start.7 = (f32[2,256]{1,0:T(2,128)S(1)}, f32[2,256]{1,0:T(2,128)}, u32[]{:S(2)}) copy-start(f32[2,256]{1,0:T(2,128)} %param.14) | copy-start | bytes 6148
  7.2 1.4 copy-start.5
  7.2 1.4 copy-start.11
  7.2 157.1 %all-gather.3.cloned.1.call-start = ((), (), s32[]{:S(2)}) async-start(), calls=%async_computation.3 | async-start | bytes 4259840 | tf_op jit(solution)/shard_map/all_gather | solution.py:82
  15.0 165.8 %all-to-all-start = ((s32[64,1,16]{2,1,0:T(1,128)}), s32[64,1,16]{2,1,0:T(1,128)S(1)}, u32[]{:S(2)}, u32[]{:S(2)}) async-start(s32[64,1,16]{2,1,0:T(1,128)} %bitcast.3), calls=%async_computation | async-start | bytes 65536 | tf_op jit(solution)/shard_map/all_to_all | solution.py:84
  168.6 1.9 copy-start.9
  168.6 1.9 copy-start.10
  172.9 2.0 copy-start.8
  177.3 132.9 %copy-start.3 = (bf16[128,256]{1,0:T(8,128)(2,1)S(1)}, bf16[128,256]{1,0:T(8,128)(2,1)}, u32[]{:S(2)}) copy-start(bf16[128,256]{1,0:T(8,128)(2,1)} %gather_fusion) | copy-start | bytes 196612
  180.9 44.3 %all-to-all-start.1 = ((bf16[64,16,256]{2,1,0:T(8,128)(2,1)}), bf16[64,16,256]{2,1,0:T(8,128)(2,1)}, u32[]{:S(2)}, u32[]{:S(2)}) async-start(bf16[64,16,256]{2,1,0:T(8,128)(2,1)} %bitcast.43), calls=%async_computation.1 | async-start | bytes 1048576 | tf_op jit(solution)/shard_map/all_to_all | solution.py:105
  191.7 116.5 %all-reduce.2.cloned.1.call-start = ((), (), s32[]{:S(2)}) async-start(), calls=%async_computation.2 | async-start | bytes 262144 | tf_op jit(solution)/shard_map/psum | solution.py:116
  310.2 2.1 copy-start.1
  312.3 1.0 copy-start.2
Sparse Core Ops, SparseCore 0:
  11.3 152.9 all-gather.2
  227.5 80.6 all-reduce.1
where the time goes:
time: 321 us; the launch traced here: 320 us
  waiting for transfers between devices  242 us (75%)
  starting transfers between devices  29.5 us (9%)
  local copies, waits for them, and re-layouts  17.8 us (6%)
  between operations  14.4 us (4%)
  matrix products  10.8 us (3%)
  other arithmetic  5.35 us (2%)
    all_gather x1, waiting for transfers between devices, on_device(): every_block = lax.all_gather(local_block, 'mp', axis=0, tiled=True)  131 us
    psum x1, waiting for transfers between devices, on_device(): grad_total = lax.psum(grad_block, 'replica')  79.6 us
    all_to_all x1, waiting for transfers between devices, on_device(): lax.all_to_all(outgoing, 'mp', split_axis=0, concat_axis=0, tiled=True)  32.1 us
    all_to_all x1, starting transfers between devices, on_device(): lax.all_to_all(requests, 'mp', split_axis=0, concat_axis=0, tiled=True)  18.6 us
    all_to_all x1, starting transfers between devices, on_device(): lax.all_to_all(outgoing, 'mp', split_axis=0, concat_axis=0, tiled=True)  10.8 us
  transfers between devices with their start and end apart: 4, of which 3 were waited for; matrix products, arithmetic and copies ran while one was open for 7% of the time, Pallas kernels for 0%

commit v1 on v0

--- a/solution.py
+++ b/solution.py
@@ -4,6 +4,12 @@
 from jax.sharding import PartitionSpec as P
 
 learn_rate = 1.0
+
+
+def gather_and_add(x, axis):
+    parts = lax.all_gather(x, axis, axis=0, tiled=False)
+    total = parts.sum(axis=0)
+    return total
 
 
 def silu_slope(values):
@@ -113,7 +119,7 @@
         preferred_element_type=jnp.float32,
     )
     touched_acc = accumulator[touched]
-    grad_total = lax.psum(grad_block, "replica")
+    grad_total = gather_and_add(grad_block, "replica")
     new_rows, new_acc = adagrad_rows(grad_total, local_block, touched_acc)
     table_out = embed_table.at[touched].set(new_rows.astype(jnp.bfloat16))
     accum_out = accumulator.at[touched].set(new_acc)

time: 321 us -> 279 us (0.87)
  waiting for transfers between devices: 242 us -> 201 us
    psum x1 -> x0, waiting for transfers between devices: 79.6 us -> none  [on_device(): grad_total = lax.psum(grad_block, 'replica')]
    all_gather x0 -> x1, waiting for transfers between devices: none -> 38.7 us  [gather_and_add(): parts = lax.all_gather(x, axis, axis=0, tiled=False)]
  transfers between devices with their start and end apart: 4 -> 4, of which waited for: 3 -> 3; matrix products, arithmetic and copies ran while one was open for 7% -> 8% of each run, Pallas kernels for 0% -> 0%
where the time goes in v1:
time: 279 us
  waiting for transfers between devices  201 us (72%)
  starting transfers between devices  29.5 us (11%)
  local copies, waits for them, and re-layouts  17.5 us (6%)
  between operations  14.4 us (5%)
  matrix products  10.8 us (4%)
  other arithmetic  5.38 us (2%)
    all_gather x1, waiting for transfers between devices, on_device(): every_block = lax.all_gather(local_block, 'mp', axis=0, tiled=True)  131 us
    all_gather x1, waiting for transfers between devices, gather_and_add(): parts = lax.all_gather(x, axis, axis=0, tiled=False)  38.7 us
    all_to_all x1, waiting for transfers between devices, on_device(): lax.all_to_all(outgoing, 'mp', split_axis=0, concat_axis=0, tiled=True)  32.1 us
    all_to_all x1, starting transfers between devices, on_device(): lax.all_to_all(requests, 'mp', split_axis=0, concat_axis=0, tiled=True)  18.6 us
    all_to_all x1, starting transfers between devices, on_device(): lax.all_to_all(outgoing, 'mp', split_axis=0, concat_axis=0, tiled=True)  10.8 us
  transfers between devices with their start and end apart: 4, of which 3 were waited for; matrix products, arithmetic and copies ran while one was open for 8% of the time, Pallas kernels for 0%

profile of v1, /device:TPU:4, one launch (start us, length us, event | category | flops | bytes accessed | tf_op | source)
XLA Modules:
  0.0 278.8 jit_solution(3459734305210951500)
XLA Ops:
  7.3 1.4 copy.27
  8.7 1.5 gather_fusion
  10.3 1.2 reduce-window.6
  11.9 2.4 scatter_custom_fusion
  14.3 0.7 all_to_all.9
  15.0 18.6 %all-to-all-start = ((s32[64,1,16]{2,1,0:T(1,128)}), s32[64,1,16]{2,1,0:T(1,128)S(1)}, u32[]{:S(2)}, u32[]{:S(2)}) async-start(s32[64,1,16]{2,1,0:T(1,128)} %bitcast.3), calls=%async_computation | async-start | bytes 65536 | tf_op jit(solution)/shard_map/all_to_all | solution.py:90
  33.8 130.6 %all-gather.5.cloned.1.call-done = bf16[8192,256]{1,0:T(8,128)(2,1)} async-done(((bf16[128,256]{1,0:T(8,128)(2,1)}), bf16[8192,256]{1,0:T(8,128)(2,1)}) %all-gather.5.cloned.1.call-update) | async-done | bytes 4194320 | tf_op jit(solution)/shard_map/all_gather | solution.py:88
  164.3 4.3 %gather_fusion.1 = bf16[512,256]{1,0:T(8,128)(2,1)S(1)} fusion(bf16[8192,256]{1,0:T(8,128)(2,1)} %all-gather.5.cloned.1.call-done, s32[1024]{0:T(1024)S(1)} %pad_clamp_fusion), kind=kCustom, calls=%fused_computation.1 | custom fusion | bytes 526336 | tf_op jit(solution)/shard_map/gather | solution.py:89
  168.6 1.9 multiply_reduce_fusion.2
  170.6 2.3 multiply_reduce_fusion.1
  172.9 2.0 multiply_reduce_fusion
  174.9 2.4 convolution_convert_fusion
  177.3 3.5 %scatter_custom_fusion.1 = bf16[1024,256]{1,0:T(8,128)(2,1)} fusion(s32[512]{0:T(512)S(1)} %bitcast.55, bf16[512,256]{1,0:T(8,128)(2,1)} %convolution_convert_fusion, bf16[]{:T(256)} %constant.35.clone.1), kind=kCustom, calls=%fused_computation.30 | custom fusion | bytes 524800 | tf_op jit(solution)/shard_map/scatter | solution.py:108
  180.9 10.8 %all-to-all-start.1 = ((bf16[64,16,256]{2,1,0:T(8,128)(2,1)}), bf16[64,16,256]{2,1,0:T(8,128)(2,1)}, u32[]{:S(2)}, u32[]{:S(2)}) async-start(bf16[64,16,256]{2,1,0:T(8,128)(2,1)} %bitcast.44), calls=%async_computation.1 | async-start | bytes 1048576 | tf_op jit(solution)/shard_map/all_to_all | solution.py:111
  191.7 0.5 broadcast.180
  192.2 0.7 reduce.5
  193.1 32.1 %all-to-all-done.1 = bf16[64,16,256]{2,1,0:T(8,128)(2,1)} async-done(((bf16[64,16,256]{2,1,0:T(8,128)(2,1)}), bf16[64,16,256]{2,1,0:T(8,128)(2,1)}, u32[]{:S(2)}, u32[]{:S(2)}) %all-to-all-start.1) | async-done | bytes 524320 | tf_op jit(solution)/shard_map/all_to_all | solution.py:111
  225.2 2.2 fusion.14
  227.4 1.1 gather_fusion.2
  228.5 38.7 %all-gather.7.cloned.1.call-done = f32[1024,256]{1,0:T(8,128)} async-done(((f32[128,256]{1,0:T(8,128)}), f32[1024,256]{1,0:T(8,128)}) %all-gather.7.cloned.1.call-update) | async-done | bytes 1048592 | tf_op jit(solution)/shard_map/all_gather | solution.py:10
  267.2 1.3 reduce_sum.64
  268.6 1.7 scatter_custom_fusion.2
  270.4 1.0 scatter_fusion
  271.4 0.6 copy-done.1
  (56 shorter events, 1.0 us)
Async XLA Ops:
  7.2 163.4 %copy-start = (bf16[1024,1024]{1,0:T(8,128)(2,1)S(1)}, bf16[1024,1024]{1,0:T(8,128)(2,1)}, u32[]{:S(2)}) copy-start(bf16[1024,1024]{1,0:T(8,128)(2,1)} %param.19) | copy-start | bytes 6291460
  7.2 3.0 %copy-start.4 = (s32[2,256]{1,0:T(2,128)S(1)}, s32[2,256]{1,0:T(2,128)}, u32[]{:S(2)}) copy-start(s32[2,256]{1,0:T(2,128)} %param.11) | copy-start | bytes 6148
  7.2 3.0 %copy-start.6 = (s32[2,256]{1,0:T(2,128)S(1)}, s32[2,256]{1,0:T(2,128)}, u32[]{:S(2)}) copy-start(s32[2,256]{1,0:T(2,128)} %param.12) | copy-start | bytes 6148
  7.2 26.4 %copy-start.12 = (s32[2]{0:T(128)S(1)}, s32[2]{0:T(128)}, u32[]{:S(2)}) copy-start(s32[2]{0:T(128)} %param.13) | copy-start | bytes 28
  7.2 26.5 %copy-start.7 = (f32[2,256]{1,0:T(2,128)S(1)}, f32[2,256]{1,0:T(2,128)}, u32[]{:S(2)}) copy-start(f32[2,256]{1,0:T(2,128)} %param.14) | copy-start | bytes 6148
  7.2 1.4 copy-start.5
  7.2 1.4 copy-start.11
  7.2 157.1 %all-gather.5.cloned.1.call-start = ((), (), s32[]{:S(2)}) async-start(), calls=%async_computation.2 | async-start | bytes 4259840 | tf_op jit(solution)/shard_map/all_gather | solution.py:88
  15.0 165.8 %all-to-all-start = ((s32[64,1,16]{2,1,0:T(1,128)}), s32[64,1,16]{2,1,0:T(1,128)S(1)}, u32[]{:S(2)}, u32[]{:S(2)}) async-start(s32[64,1,16]{2,1,0:T(1,128)} %bitcast.3), calls=%async_computation | async-start | bytes 65536 | tf_op jit(solution)/shard_map/all_to_all | solution.py:90
  168.6 1.9 copy-start.9
  168.6 1.9 copy-start.10
  172.9 2.0 copy-start.8
  177.3 91.3 %copy-start.3 = (bf16[128,256]{1,0:T(8,128)(2,1)S(1)}, bf16[128,256]{1,0:T(8,128)(2,1)}, u32[]{:S(2)}) copy-start(bf16[128,256]{1,0:T(8,128)(2,1)} %gather_fusion) | copy-start | bytes 196612
  180.9 44.3 %all-to-all-start.1 = ((bf16[64,16,256]{2,1,0:T(8,128)(2,1)}), bf16[64,16,256]{2,1,0:T(8,128)(2,1)}, u32[]{:S(2)}, u32[]{:S(2)}) async-start(bf16[64,16,256]{2,1,0:T(8,128)(2,1)} %bitcast.44), calls=%async_computation.1 | async-start | bytes 1048576 | tf_op jit(solution)/shard_map/all_to_all | solution.py:111
  191.7 75.5 %all-gather.7.cloned.1.call-start = ((), (), s32[]{:S(2)}) async-start(), calls=%async_computation.3 | async-start | bytes 1179648 | tf_op jit(solution)/shard_map/all_gather | solution.py:10
  270.4 1.0 copy-start.2
  271.4 0.6 copy-start.1
Sparse Core Ops, SparseCore 0:
  11.3 152.9 all-gather.4
  227.5 39.6 all-gather.6
